TPU v7x, 128 devices: a whole 4x4x4 slice. The times are simulated.
128 devices in a mesh: seq: 16 (over y, z), store: 8 (over x, core).
Axes of the slice: x: 4, y: 4, z: 4, core: 2. Of those that a mesh axis runs over, the one named last changes fastest.
Arguments:
- hidden: bfloat16 [16384, 4096], P('seq'), may hold values from -6 to 6
- nbr_table: bfloat16 [64, 128, 896], P('store'), may hold values from -6 to 6
- nbr_ids: int32 [256, 2], P('seq'), may hold values from 0 to 63, as said below
- w_query: bfloat16 [4096, 4096], P(None, 'store'), may hold values from -0.09375 to 0.09375
- w_key: bfloat16 [896, 4096], P(None, 'store'), may hold values from -0.1875 to 0.1875
- w_value: bfloat16 [896, 4096], P(None, 'store'), may hold values from -0.1875 to 0.1875
- w_out: bfloat16 [4096, 4096], P('store'), may hold values from -0.125 to 0.125
- enc_query: bfloat16 [896, 896], replicated, may hold values from -0.1875 to 0.1875
- enc_key: bfloat16 [4096, 896], P('seq'), may hold values from -0.09375 to 0.09375
- enc_value: bfloat16 [4096, 896], P('seq'), may hold values from -0.09375 to 0.09375
- enc_out: bfloat16 [896, 896], replicated, may hold values from -0.1875 to 0.1875
Outputs:
- cross_out: bfloat16 [16384, 4096], P('seq', 'store')
Inputs may be any that keep to these rules, and one draw needn't show every extreme that they name: `nbr_ids`: among the spans of one index of seq (16 consecutive spans), the ids fall in each owner's range k * 8 to k * 8 + 7 exactly 4 times.
All inputs are finite; a program needn't handle non-finite values.
Results may differ from a plain program's by a relative error of at most 0.03.
Values may be sent and summed in bfloat16 or wider, within the bound.
No kernel may reach another device: no remote copies, remote signals or barrier semaphores. Data moves between devices by JAX's collectives and lax.ppermute only.
A program may use at most 128 MiB of HBM per device.

v0:
```python
import math
import jax
import jax.numpy as jnp
from jax import lax
from jax.sharding import PartitionSpec as P

D = 4096
HD = 128
E = 896
EHEADS = 14
EHD = 64
CH = 64
NLEN = 128
KNB = 2
EPSILON = 1e-06


def shifted(block, axis, distance):
    devices = range(lax.axis_size(axis))
    route = [(i - distance, i) for i in devices if i - distance in devices]
    return lax.ppermute(block, axis, route)


def encoder_block(sources, cond_keys, cond_values, enc_query, enc_out):
    count = sources.shape[0]
    source_f = sources.astype(jnp.float32)
    normed = (
        source_f * lax.rsqrt(jnp.mean(source_f * source_f, axis=-1, keepdims=True) + EPSILON)
    ).astype(jnp.bfloat16)
    queries = jnp.dot(
        normed.reshape(count * NLEN, E), enc_query, preferred_element_type=jnp.float32
    ).astype(jnp.bfloat16)
    queries = queries.reshape(count, NLEN, EHEADS, EHD)
    key_heads = cond_keys.reshape(count, CH, EHEADS, EHD)
    value_heads = cond_values.reshape(count, CH, EHEADS, EHD)
    scores = jnp.einsum(
        "nqhd,nkhd->nhqk", queries, key_heads, preferred_element_type=jnp.float32
    ) / math.sqrt(EHD)
    weights = jax.nn.softmax(scores, axis=-1).astype(jnp.bfloat16)
    mixed_heads = jnp.einsum(
        "nhqk,nkhd->nqhd", weights, value_heads, preferred_element_type=jnp.float32
    ).astype(jnp.bfloat16)
    branch = jnp.dot(
        mixed_heads.reshape(count * NLEN, E), enc_out, preferred_element_type=jnp.float32
    )
    return (source_f + branch.reshape(count, NLEN, E)).astype(jnp.bfloat16)


def body(
    hidden,
    nbr_table,
    nbr_ids,
    w_query,
    w_key,
    w_value,
    w_out,
    enc_query,
    enc_key,
    enc_value,
    enc_out,
):
    store_count = lax.axis_size("store")
    store_rank = lax.axis_index("store")
    span_count = nbr_ids.shape[0]
    row_requests = span_count * KNB
    per_owner = row_requests // store_count
    blocks_here = nbr_table.shape[0]
    token_count = hidden.shape[0]
    flat_ids = nbr_ids.reshape(-1)
    owners = flat_ids // blocks_here
    slot_index = jnp.arange(row_requests, dtype=jnp.int32)
    by_owner = jnp.sort(owners * row_requests + slot_index) % row_requests
    picked = lax.dynamic_slice_in_dim(by_owner, store_rank * per_owner, per_owner)
    sources = nbr_table[flat_ids[picked] % blocks_here]
    span_of = picked // KNB
    by_span = hidden.reshape(span_count, CH, D)
    condition = by_span[span_of].reshape(per_owner * CH, D)
    shard_rows = (
        lax.all_gather(enc_key, "seq", axis=0, tiled=True),
        lax.all_gather(enc_value, "seq", axis=0, tiled=True),
    )
    key_sum = jnp.dot(condition, shard_rows[0], preferred_element_type=jnp.float32)
    value_sum = jnp.dot(condition, shard_rows[1], preferred_element_type=jnp.float32)
    cond_keys = key_sum.astype(jnp.bfloat16).reshape(per_owner, CH, E)
    cond_values = value_sum.astype(jnp.bfloat16).reshape(per_owner, CH, E)
    encoded = encoder_block(sources, cond_keys, cond_values, enc_query, enc_out)
    head_width = w_query.shape[1]
    shard_rows = lax.all_gather(encoded, "store", axis=0, tiled=True)
    flat_rows = shard_rows.reshape(-1, E)
    keys_part = jnp.dot(flat_rows, w_key, preferred_element_type=jnp.float32).astype(jnp.bfloat16)
    values_part = jnp.dot(flat_rows, w_value, preferred_element_type=jnp.float32).astype(
        jnp.bfloat16
    )
    joined = jnp.concatenate([keys_part, values_part], axis=1)
    owner_order = joined.reshape(shard_rows.shape[0], NLEN, 2 * head_width)
    key_value = owner_order[jnp.argsort(by_owner)].reshape(span_count, KNB * NLEN, 2 * head_width)
    carried = shifted(key_value[span_count - 1], "seq", 1)
    previous = jnp.concatenate([carried[None], key_value[: span_count - 1]], axis=0)
    local_heads = head_width // HD
    queries = jnp.dot(hidden, w_query, preferred_element_type=jnp.float32).astype(jnp.bfloat16)
    queries = queries.reshape(span_count, CH, local_heads, HD)
    key_heads = previous[:, :, :head_width].reshape(span_count, KNB * NLEN, local_heads, HD)
    value_heads = previous[:, :, head_width:].reshape(span_count, KNB * NLEN, local_heads, HD)
    scores = jnp.einsum(
        "cqhd,ckhd->chqk", queries, key_heads, preferred_element_type=jnp.float32
    ) / math.sqrt(HD)
    weights = jax.nn.softmax(scores, axis=-1).astype(jnp.bfloat16)
    attended = jnp.einsum(
        "chqk,ckhd->cqhd", weights, value_heads, preferred_element_type=jnp.float32
    )
    attended = attended.astype(jnp.bfloat16).reshape(token_count, head_width)
    head_terms = jnp.dot(attended, w_out, preferred_element_type=jnp.float32)
    return lax.psum_scatter(
        head_terms.astype(jnp.bfloat16), "store", scatter_dimension=1, tiled=True
    )


def solution(mesh):
    in_specs = (
        P("seq", None),
        P("store", None, None),
        P("seq", None),
        P(None, "store"),
        P(None, "store"),
        P(None, "store"),
        P("store", None),
        P(),
        P("seq", None),
        P("seq", None),
        P(),
    )
    out_specs = P("seq", "store")
    return jax.shard_map(body, mesh=mesh, in_specs=in_specs, out_specs=out_specs, check_vma=False)
```

profile of v0, /device:TPU:1, one launch (start us, length us, event | category | flops | bytes accessed | tf_op | source)
XLA Modules:
  0.0 372.8 jit_solution(12636594940149134104)
XLA Ops:
  6.5 0.0 copy-start
  6.5 0.0 all-gather.6.cloned.1.call-start
  6.5 0.7 all-gather.6.cloned.1.call-update
  7.3 0.0 all-gather.4.cloned.1.call-start
  7.3 0.7 all-gather.4.cloned.1.call-update
  8.0 0.0 all-gather.8.cloned.1.call-start
  8.1 0.8 copy.34
  8.8 0.1 reshape.108
  8.9 1.6 sort.32
  10.5 0.1 compare_select_fusion.10
  10.6 0.6 gather_fusion
  11.3 0.0 copy-done
  11.3 0.7 gather_fusion.1
  12.0 0.3 multiply_reduce_fusion.1
  12.3 0.2 fusion.10
  12.5 2.6 convolution_convert_fusion.4
  15.1 2.4 reshape.156
  17.6 5.4 %gather_fusion.2 = bf16[4,64,4096]{2,1,0:T(8,128)(2,1)} fusion(bf16[16,64,4096]{2,1,0:T(8,128)(2,1)} %bitcast.59, s32[1024]{0:T(1024)S(1)} %get-tuple-element.14), kind=kCustom, calls=%fused_computation.2 | custom fusion | bytes 4194320 | tf_op jit(solution)/shard_map/gather | solution.py:77
  23.0 56.1 %all-gather.6.cloned.1.call-done = bf16[4096,896]{1,0:T(8,128)(2,1)} async-done(((bf16[256,896]{1,0:T(8,128)(2,1)}), bf16[4096,896]{1,0:T(8,128)(2,1)}) %all-gather.6.cloned.1.call-update) | async-done | bytes 7340048 | tf_op jit(solution)/shard_map/all_gather | solution.py:79
  79.1 6.1 %convolution_convert_fusion.6 = bf16[256,896]{1,0:T(8,128)(2,1)S(1)} fusion(bf16[256,4096]{1,0:T(8,128)(2,1)} %bitcast.54, bf16[4096,896]{1,0:T(8,128)(2,1)} %all-gather.6.cloned.1.call-done), kind=kOutput, calls=%fused_computation.37 | convolution fusion | flops 1879277568 | bytes 9895936 | tf_op jit(solution)/shard_map/dot_general | solution.py:82
  85.1 0.7 reshape.157
  85.8 2.9 fusion.8
  88.7 0.0 copy-start.3
  88.7 1.3 copy-done.3
  90.0 0.5 fusion.45
  90.5 56.6 %all-gather.4.cloned.1.call-done = bf16[4096,896]{1,0:T(8,128)(2,1)} async-done(((bf16[256,896]{1,0:T(8,128)(2,1)}), bf16[4096,896]{1,0:T(8,128)(2,1)}) %all-gather.4.cloned.1.call-update) | async-done | bytes 7340048 | tf_op jit(solution)/shard_map/all_gather | solution.py:80
  147.1 6.1 %convolution_convert_fusion.7 = bf16[256,896]{1,0:T(8,128)(2,1)S(1)} fusion(bf16[256,4096]{1,0:T(8,128)(2,1)} %bitcast.55, bf16[4096,896]{1,0:T(8,128)(2,1)} %all-gather.4.cloned.1.call-done), kind=kOutput, calls=%fused_computation.38 | convolution fusion | flops 1879277568 | bytes 9895936 | tf_op jit(solution)/shard_map/dot_general | solution.py:83
  153.2 1.7 reshape.155
  154.8 0.0 copy-start.4
  154.8 3.7 convolution_convert_fusion.5
  158.6 0.0 copy-done.4
  158.6 3.4 add_convert_fusion
  161.9 0.0 all-gather.8.cloned.1.call-update
  161.9 0.2 reduce-scatter.2.cloned.1.call-start
  162.2 1.7 sort.33
  163.9 43.5 %all-gather.8.cloned.1.call-done = bf16[32,128,896]{2,1,0:T(8,128)(2,1)} async-done(((bf16[4,128,896]{2,1,0:T(8,128)(2,1)}), bf16[32,128,896]{2,1,0:T(8,128)(2,1)}) %all-gather.8.cloned.1.call-update) | async-done | bytes 7340048 | tf_op jit(solution)/shard_map/all_gather | solution.py:88
  207.4 0.0 copy-start.5
  207.4 9.9 %convolution_convert_fusion.1 = bf16[4096,512]{0,1:T(8,128)(2,1)} fusion(bf16[4096,896]{1,0:T(8,128)(2,1)} %bitcast.60, bf16[896,512]{1,0:T(8,128)(2,1)} %param.16), kind=kOutput, calls=%fused_computation.10 | convolution fusion | flops 3760193536 | bytes 12451840 | tf_op jit(solution)/shard_map/dot_general | solution.py:91
  217.4 0.0 copy-done.5
  217.4 0.0 copy-done.6
  217.4 6.3 %convolution_convert_fusion.2 = bf16[4096,512]{0,1:T(8,128)(2,1)} fusion(bf16[4096,896]{1,0:T(8,128)(2,1)S(1)} %bitcast.61, bf16[896,512]{1,0:T(8,128)(2,1)S(1)} %copy-done.6), kind=kOutput, calls=%fused_computation.11 | convolution fusion | flops 3760193536 | bytes 12451840 | tf_op jit(solution)/shard_map/dot_general | solution.py:90
  223.6 7.8 %pad_maximum_fusion = bf16[4096,1024]{0,1:T(8,128)(2,1)} fusion(bf16[4096,512]{0,1:T(8,128)(2,1)} %convolution_convert_fusion.1, bf16[4096,512]{0,1:T(8,128)(2,1)} %convolution_convert_fusion.2), kind=kLoop, calls=%fused_computation.6 | loop fusion | flops 16777216 | bytes 16777216 | tf_op jit(solution)/shard_map/concatenate | solution.py:94
  231.4 11.9 %copy.58 = bf16[4096,1024]{1,0:T(8,128)(2,1)} copy(bf16[4096,1024]{0,1:T(8,128)(2,1)} %pad_maximum_fusion) | data formatting | bytes 16777216 | tf_op jit(solution)/shard_map/reshape | solution.py:95
  243.3 8.4 %gather_fusion.3 = bf16[32,128,1024]{2,1,0:T(8,128)(2,1)} fusion(bf16[32,128,1024]{2,1,0:T(8,128)(2,1)} %bitcast.51, s32[1024]{0:T(1024)S(1)} %pad_clamp_fusion), kind=kCustom, calls=%fused_computation.3 | custom fusion | bytes 16777344 | tf_op jit(solution)/shard_map/gather | solution.py:96
  251.7 1.9 slice.29
  253.6 3.2 collective-permute-start
  256.8 9.1 %convolution_convert_fusion.3 = bf16[1024,512]{1,0:T(8,128)(2,1)S(1)} fusion(bf16[1024,4096]{1,0:T(8,128)(2,1)} %param.11, bf16[4096,512]{1,0:T(8,128)(2,1)} %param.14), kind=kOutput, calls=%fused_computation.33 | convolution fusion | flops 4295491584 | bytes 13631488 | tf_op jit(solution)/shard_map/dot_general | solution.py:100
  265.9 0.5 reshape.115
  266.4 0.0 slice-start
  266.4 1.8 collective-permute-done
  268.1 1.5 slice-done
  269.6 3.7 pad_maximum_fusion.1
  273.3 6.4 %copy.44 = bf16[16,256,512]{1,2,0:T(8,128)(2,1)} copy(bf16[16,256,512]{2,1,0:T(8,128)(2,1)} %get-tuple-element.10) | data formatting | bytes 8388608 | tf_op jit(solution)/shard_map/slice | solution.py:102
  279.7 2.9 fusion.20
  282.6 0.0 copy-start.2
  282.6 2.0 copy-done.2
  284.6 1.6 fusion.46
  286.1 6.4 %copy.43 = bf16[16,256,512]{1,2,0:T(8,128)(2,1)} copy(bf16[16,256,512]{2,1,0:T(8,128)(2,1)} %get-tuple-element.11) | data formatting | bytes 8388608 | tf_op jit(solution)/shard_map/slice | solution.py:103
  292.5 11.9 %fusion.17 = bf16[16,64,4,128]{3,1,2,0:T(8,128)(2,1)S(1)} fusion(bf16[16,256,4,128]{1,3,2,0:T(8,128)(2,1)} %bitcast.53, f32[16,4,64]{2,1,0:T(4,128)S(1)} %fusion.46, f32[16,4,64,256]{3,2,1,0:T(8,128)} %copy-done.2), kind=kOutput, calls=%fused_computation.36 | convolution fusion | flops 274206976 | bytes 9453568 | tf_op jit(solution)/shard_map/chqk,ckhd->cqhd/dot_general | solution.py:108
  304.5 0.9 copy.48
  305.4 8.9 %convolution_convert_fusion = bf16[1024,4096]{1,0:T(8,128)(2,1)} fusion(bf16[512,4096]{1,0:T(8,128)(2,1)} %param.17, bf16[128,8,4,128]{3,2,1,0:T(4,128)(2,1)S(1)} %bitcast.56), kind=kOutput, calls=%fused_computation.9 | convolution fusion | flops 4299161600 | bytes 13631488 | tf_op jit(solution)/shard_map/dot_general | solution.py:112
  314.3 0.0 reduce-scatter.2.cloned.1.call-update
  314.3 51.9 %reduce-scatter.2.cloned.1.call-done = bf16[1024,512]{1,0:T(8,128)(2,1)} async-done(((bf16[1024,4096]{1,0:T(8,128)(2,1)}), bf16[1024,512]{1,0:T(8,128)(2,1)}) %reduce-scatter.2.cloned.1.call-update) | async-done | bytes 1048592 | tf_op jit(solution)/shard_map/reduce_scatter | solution.py:113
  366.2 0.0 copy-done.1
  (12 shorter events, 0.1 us)
Async XLA Ops:
  6.5 4.8 %copy-start = (bf16[8,128,896]{2,1,0:T(8,128)(2,1)S(1)}, bf16[8,128,896]{2,1,0:T(8,128)(2,1)}, u32[]{:S(2)}) copy-start(bf16[8,128,896]{2,1,0:T(8,128)(2,1)} %param.12) | copy-start | bytes 5505028
  6.5 72.5 %all-gather.6.cloned.1.call-start = ((), (), s32[]{:S(2)}) async-start(), calls=%async_computation.2 | async-start | bytes 7798784 | tf_op jit(solution)/shard_map/all_gather | solution.py:79
  7.3 139.9 %all-gather.4.cloned.1.call-start = ((), (), s32[]{:S(2)}) async-start(), calls=%async_computation.1 | async-start | bytes 7798784 | tf_op jit(solution)/shard_map/all_gather | solution.py:80
  8.0 199.4 %all-gather.8.cloned.1.call-start = ((), (), s32[]{:S(2)}) async-start(), calls=%async_computation.3 | async-start | bytes 8257536 | tf_op jit(solution)/shard_map/all_gather | solution.py:88
  88.7 1.3 copy-start.3
  154.8 3.7 copy-start.4
  161.9 204.3 %reduce-scatter.2.cloned.1.call-start = ((), (), s32[]{:S(2)}) async-start(), calls=%async_computation.4 | async-start | bytes 9437184 | tf_op jit(solution)/shard_map/reduce_scatter | solution.py:113
  207.4 10.0 %copy-start.5 = (bf16[32,128,896]{2,1,0:T(8,128)(2,1)S(1)}, bf16[32,128,896]{2,1,0:T(8,128)(2,1)}, u32[]{:S(2)}) copy-start(bf16[32,128,896]{2,1,0:T(8,128)(2,1)} %all-gather.8.cloned.1.call-done) | copy-start | bytes 22020100
  207.4 10.0 %copy-start.6 = (bf16[896,512]{1,0:T(8,128)(2,1)S(1)}, bf16[896,512]{1,0:T(8,128)(2,1)}, u32[]{:S(2)}) copy-start(bf16[896,512]{1,0:T(8,128)(2,1)} %param.15) | copy-start | bytes 2752516
  253.6 14.5 %collective-permute-start = (bf16[256,1024]{1,0:T(8,128)(2,1)}, bf16[256,1024]{1,0:T(8,128)(2,1)S(1)}, u32[]{:S(2)}, u32[]{:S(2)}) collective-permute-start(bf16[256,1024]{1,0:T(8,128)(2,1)} %bitcast.11), channel_id=1, source_target_pairs={{0,8},{8,16},{16,24},{24,32},{32,40},{40,48},{48,56},{56,64},{64,7... | collective-permute-start | bytes 1572872 | tf_op jit(solution)/shard_map/ppermute | solution.py:21
  266.4 3.2 slice-start
  282.6 2.0 copy-start.2
  314.3 51.9 %copy-start.1 = (bf16[8,128,896]{2,1,0:T(8,128)(2,1)S(1)}, bf16[8,128,896]{2,1,0:T(8,128)(2,1)}, u32[]{:S(2)}) copy-start(bf16[8,128,896]{2,1,0:T(8,128)(2,1)} %param.12) | copy-start | bytes 5505028
Sparse Core Ops, SparseCore 0:
  9.5 69.4 all-gather.5
  81.2 65.8 all-gather.3
  162.1 45.3 all-gather.7
  314.5 51.7 reduce-scatter.1
where the time goes:
time: 374 us; the launch traced here: 373 us
  waiting for transfers between devices  211 us (56%)
  matrix products  73.7 us (20%)
  local copies, waits for them, and re-layouts  53.5 us (14%)
  other arithmetic  17.5 us (5%)
  between operations  13.3 us (4%)
    all_gather x1, waiting for transfers between devices, body(): lax.all_gather(enc_value, 'seq', axis=0, tiled=True)  56.6 us
    all_gather x1, waiting for transfers between devices, body(): lax.all_gather(enc_key, 'seq', axis=0, tiled=True)  56.1 us
    reduce_scatter x1, waiting for transfers between devices, body(): lax.psum_scatter(head_terms.astype(jnp.bfloat16), 'store', scatter_dimens...  51.9 us
    all_gather x1, waiting for transfers between devices, body(): shard_rows = lax.all_gather(encoded, 'store', axis=0, tiled=True)  43.5 us
    dot_general x1, matrix products, body(): jnp.einsum('chqk,ckhd->cqhd', weights, value_heads, preferred_element_typ...  11.9 us
    reshape x1, local copies, waits for them, and re-layouts, body(): owner_order = joined.reshape(shard_rows.shape[0], NLEN, 2 * head_width)  11.9 us
    dot_general x1, matrix products, body(): jnp.dot(flat_rows, w_value, preferred_element_type=jnp.float32)  9.94 us
    dot_general x1, matrix products, body(): jnp.dot(hidden, w_query, preferred_element_type=jnp.float32)  9.05 us
  transfers between devices with their start and end apart: 5, of which 5 were waited for; matrix products, arithmetic and copies ran while one was open for 10% of the time, Pallas kernels for 0%

commit v1 on v0

--- a/solution.py
+++ b/solution.py
@@ -85,7 +85,9 @@
     cond_values = value_sum.astype(jnp.bfloat16).reshape(per_owner, CH, E)
     encoded = encoder_block(sources, cond_keys, cond_values, enc_query, enc_out)
     head_width = w_query.shape[1]
-    shard_rows = lax.all_gather(encoded, "store", axis=0, tiled=True)
+    shard_rows = jnp.concatenate(
+        lax.all_to_all(jnp.stack([encoded] * lax.axis_size("store")), "store", 0, 0), axis=0
+    )
     flat_rows = shard_rows.reshape(-1, E)
     keys_part = jnp.dot(flat_rows, w_key, preferred_element_type=jnp.float32).astype(jnp.bfloat16)
     values_part = jnp.dot(flat_rows, w_value, preferred_element_type=jnp.float32).astype(

time: 374 us -> 420 us (1.12)
  waiting for transfers between devices: 211 us -> 247 us
  starting transfers between devices: 3.49 us -> 8.56 us
    all_to_all x0 -> x1, waiting for transfers between devices: none -> 81 us  [body(): lax.all_to_all(jnp.stack([encoded] * lax.axis_size('store')), 'store', 0, 0)]
    all_gather x1 -> x0, waiting for transfers between devices: 43.5 us -> none  [body(): shard_rows = lax.all_gather(encoded, 'store', axis=0, tiled=True)]
    all_to_all x0 -> x1, starting transfers between devices: none -> 5.53 us  [body(): lax.all_to_all(jnp.stack([encoded] * lax.axis_size('store')), 'store', 0, 0)]
  transfers between devices with their start and end apart: 5 -> 5, of which waited for: 5 -> 5; matrix products, arithmetic and copies ran while one was open for 10% -> 9% of each run, Pallas kernels for 0% -> 0%
where the time goes in v1:
time: 420 us; the launch traced here: 419 us
  waiting for transfers between devices  247 us (59%)
  matrix products  75.1 us (18%)
  local copies, waits for them, and re-layouts  57.3 us (14%)
  other arithmetic  17.4 us (4%)
  between operations  13.3 us (3%)
  starting transfers between devices  8.56 us (2%)
    all_to_all x1, waiting for transfers between devices, body(): lax.all_to_all(jnp.stack([encoded] * lax.axis_size('store')), 'store', 0, 0)  81 us
    all_gather x1, waiting for transfers between devices, body(): lax.all_gather(enc_value, 'seq', axis=0, tiled=True)  56.6 us
    all_gather x1, waiting for transfers between devices, body(): lax.all_gather(enc_key, 'seq', axis=0, tiled=True)  56.1 us
    reduce_scatter x1, waiting for transfers between devices, body(): lax.psum_scatter(head_terms.astype(jnp.bfloat16), 'store', scatter_dimens...  51.3 us
    dot_general x1, matrix products, body(): jnp.einsum('chqk,ckhd->cqhd', weights, value_heads, preferred_element_typ...  11.9 us
    reshape x1, local copies, waits for them, and re-layouts, body(): owner_order = joined.reshape(shard_rows.shape[0], NLEN, 2 * head_width)  11.9 us
    dot_general x1, matrix products, body(): jnp.dot(flat_rows, w_value, preferred_element_type=jnp.float32)  9.24 us
    dot_general x1, matrix products, body(): jnp.dot(flat_rows, w_key, preferred_element_type=jnp.float32)  9.21 us
  transfers between devices with their start and end apart: 5, of which 5 were waited for; matrix products, arithmetic and copies ran while one was open for 9% of the time, Pallas kernels for 0%

profile of v1, /device:TPU:1, one launch (start us, length us, event | category | flops | bytes accessed | tf_op | source)
XLA Modules:
  0.0 419.1 jit_solution(7468678962293575318)
XLA Ops:
  6.5 0.0 copy-start
  6.5 0.0 all-gather.5.cloned.1.call-start
  6.5 0.7 all-gather.5.cloned.1.call-update
  7.3 0.0 all-gather.3.cloned.1.call-start
  7.3 0.7 all-gather.3.cloned.1.call-update
  8.0 0.8 copy.19
  8.8 0.1 reshape.107
  8.9 1.6 sort.32
  10.5 0.1 compare_select_fusion.10
  10.6 0.6 gather_fusion
  11.3 0.0 copy-done
  11.3 0.7 gather_fusion.1
  12.0 0.3 multiply_reduce_fusion.1
  12.2 0.2 fusion.10
  12.5 2.6 convolution_convert_fusion.4
  15.1 2.4 reshape.154
  17.5 5.4 %gather_fusion.2 = bf16[4,64,4096]{2,1,0:T(8,128)(2,1)} fusion(bf16[16,64,4096]{2,1,0:T(8,128)(2,1)} %bitcast.59, s32[1024]{0:T(1024)S(1)} %get-tuple-element.14), kind=kCustom, calls=%fused_computation.2 | custom fusion | bytes 4194320 | tf_op jit(solution)/shard_map/gather | solution.py:77
  22.9 56.1 %all-gather.5.cloned.1.call-done = bf16[4096,896]{1,0:T(8,128)(2,1)} async-done(((bf16[256,896]{1,0:T(8,128)(2,1)}), bf16[4096,896]{1,0:T(8,128)(2,1)}) %all-gather.5.cloned.1.call-update) | async-done | bytes 7340048 | tf_op jit(solution)/shard_map/all_gather | solution.py:79
  79.1 6.1 %convolution_convert_fusion.6 = bf16[256,896]{1,0:T(8,128)(2,1)S(1)} fusion(bf16[256,4096]{1,0:T(8,128)(2,1)} %bitcast.54, bf16[4096,896]{1,0:T(8,128)(2,1)} %all-gather.5.cloned.1.call-done), kind=kOutput, calls=%fused_computation.37 | convolution fusion | flops 1879277568 | bytes 9895936 | tf_op jit(solution)/shard_map/dot_general | solution.py:82
  85.1 0.7 reshape.155
  85.8 2.9 fusion.8
  88.7 0.0 copy-start.3
  88.7 1.3 copy-done.3
  90.0 0.5 fusion.45
  90.5 56.6 %all-gather.3.cloned.1.call-done = bf16[4096,896]{1,0:T(8,128)(2,1)} async-done(((bf16[256,896]{1,0:T(8,128)(2,1)}), bf16[4096,896]{1,0:T(8,128)(2,1)}) %all-gather.3.cloned.1.call-update) | async-done | bytes 7340048 | tf_op jit(solution)/shard_map/all_gather | solution.py:80
  147.1 6.1 %convolution_convert_fusion.7 = bf16[256,896]{1,0:T(8,128)(2,1)S(1)} fusion(bf16[256,4096]{1,0:T(8,128)(2,1)} %bitcast.55, bf16[4096,896]{1,0:T(8,128)(2,1)} %all-gather.3.cloned.1.call-done), kind=kOutput, calls=%fused_computation.38 | convolution fusion | flops 1879277568 | bytes 9895936 | tf_op jit(solution)/shard_map/dot_general | solution.py:83
  153.2 0.7 reshape.153
  153.9 3.3 convolution_convert_fusion.5
  157.1 3.0 add_convert_fusion
  160.1 4.1 stack.2
  164.2 0.0 copy-start.4
  164.2 5.5 %all-to-all-start = ((bf16[8,4,128,896]{3,2,1,0:T(8,128)(2,1)}), bf16[8,4,128,896]{3,2,1,0:T(8,128)(2,1)}, u32[]{:S(2)}, u32[]{:S(2)}) async-start(bf16[8,4,128,896]{3,2,1,0:T(8,128)(2,1)} %stack.2), calls=%async_computation | async-start | bytes 14680064 | tf_op jit(solution)/shard_map/all_to_all | solution.py:89
  169.7 0.0 reduce-scatter.2.cloned.1.call-start
  169.7 1.6 sort.33
  171.3 81.0 %all-to-all-done = bf16[8,4,128,896]{3,2,1,0:T(8,128)(2,1)} async-done(((bf16[8,4,128,896]{3,2,1,0:T(8,128)(2,1)}), bf16[8,4,128,896]{3,2,1,0:T(8,128)(2,1)}, u32[]{:S(2)}, u32[]{:S(2)}) %all-to-all-start) | async-done | bytes 7340064 | tf_op jit(solution)/shard_map/all_to_all | solution.py:89
  252.3 0.0 copy-done.4
  252.3 0.0 copy-start.5
  252.3 9.2 %convolution_convert_fusion.1 = bf16[4096,512]{0,1:T(8,128)(2,1)} fusion(bf16[4096,896]{1,0:T(8,128)(2,1)} %bitcast.9, bf16[896,512]{1,0:T(8,128)(2,1)S(1)} %copy-done.4), kind=kOutput, calls=%fused_computation.10 | convolution fusion | flops 3760193536 | bytes 12451840 | tf_op jit(solution)/shard_map/dot_general | solution.py:93
  261.6 0.0 copy-done.5
  261.6 9.2 %convolution_convert_fusion.2 = bf16[4096,512]{0,1:T(8,128)(2,1)} fusion(bf16[4096,896]{1,0:T(8,128)(2,1)} %bitcast.9, bf16[896,512]{1,0:T(8,128)(2,1)S(1)} %copy-done.5), kind=kOutput, calls=%fused_computation.11 | convolution fusion | flops 3760193536 | bytes 12451840 | tf_op jit(solution)/shard_map/dot_general | solution.py:92
  270.8 7.8 %pad_maximum_fusion = bf16[4096,1024]{0,1:T(8,128)(2,1)} fusion(bf16[4096,512]{0,1:T(8,128)(2,1)} %convolution_convert_fusion.1, bf16[4096,512]{0,1:T(8,128)(2,1)} %convolution_convert_fusion.2), kind=kLoop, calls=%fused_computation.6 | loop fusion | flops 16777216 | bytes 16777216 | tf_op jit(solution)/shard_map/concatenate | solution.py:96
  278.6 11.9 %copy.43 = bf16[4096,1024]{1,0:T(8,128)(2,1)} copy(bf16[4096,1024]{0,1:T(8,128)(2,1)} %pad_maximum_fusion) | data formatting | bytes 16777216 | tf_op jit(solution)/shard_map/reshape | solution.py:97
  290.5 8.4 %gather_fusion.3 = bf16[32,128,1024]{2,1,0:T(8,128)(2,1)} fusion(bf16[32,128,1024]{2,1,0:T(8,128)(2,1)} %bitcast.51, s32[1024]{0:T(1024)S(1)} %pad_clamp_fusion), kind=kCustom, calls=%fused_computation.3 | custom fusion | bytes 16777344 | tf_op jit(solution)/shard_map/gather | solution.py:98
  298.9 1.9 slice.29
  300.8 3.0 collective-permute-start
  303.8 9.1 %convolution_convert_fusion.3 = bf16[1024,512]{1,0:T(8,128)(2,1)S(1)} fusion(bf16[1024,4096]{1,0:T(8,128)(2,1)} %param.11, bf16[4096,512]{1,0:T(8,128)(2,1)} %param.14), kind=kOutput, calls=%fused_computation.33 | convolution fusion | flops 4295491584 | bytes 13631488 | tf_op jit(solution)/shard_map/dot_general | solution.py:102
  312.8 0.5 reshape.113
  313.4 0.0 slice-start
  313.4 1.0 collective-permute-done
  314.4 2.2 slice-done
  316.6 3.7 pad_maximum_fusion.1
  320.3 6.4 %copy.29 = bf16[16,256,512]{1,2,0:T(8,128)(2,1)} copy(bf16[16,256,512]{2,1,0:T(8,128)(2,1)} %get-tuple-element.10) | data formatting | bytes 8388608 | tf_op jit(solution)/shard_map/slice | solution.py:104
  326.7 2.9 fusion.20
  329.6 0.0 copy-start.2
  329.6 2.0 copy-done.2
  331.6 1.6 fusion.46
  333.1 6.4 %copy.28 = bf16[16,256,512]{1,2,0:T(8,128)(2,1)} copy(bf16[16,256,512]{2,1,0:T(8,128)(2,1)} %get-tuple-element.11) | data formatting | bytes 8388608 | tf_op jit(solution)/shard_map/slice | solution.py:105
  339.5 11.9 %fusion.17 = bf16[16,64,4,128]{3,1,2,0:T(8,128)(2,1)S(1)} fusion(bf16[16,256,4,128]{1,3,2,0:T(8,128)(2,1)} %bitcast.53, f32[16,4,64]{2,1,0:T(4,128)S(1)} %fusion.46, f32[16,4,64,256]{3,2,1,0:T(8,128)} %copy-done.2), kind=kOutput, calls=%fused_computation.36 | convolution fusion | flops 274206976 | bytes 9453568 | tf_op jit(solution)/shard_map/chqk,ckhd->cqhd/dot_general | solution.py:110
  351.5 0.9 copy.33
  352.4 8.9 %convolution_convert_fusion = bf16[1024,4096]{1,0:T(8,128)(2,1)} fusion(bf16[512,4096]{1,0:T(8,128)(2,1)} %param.17, bf16[128,8,4,128]{3,2,1,0:T(4,128)(2,1)S(1)} %bitcast.56), kind=kOutput, calls=%fused_computation.9 | convolution fusion | flops 4299161600 | bytes 13631488 | tf_op jit(solution)/shard_map/dot_general | solution.py:114
  361.3 0.0 copy-start.1
  361.3 0.0 reduce-scatter.2.cloned.1.call-update
  361.3 51.3 %reduce-scatter.2.cloned.1.call-done = bf16[1024,512]{1,0:T(8,128)(2,1)} async-done(((bf16[1024,4096]{1,0:T(8,128)(2,1)}), bf16[1024,512]{1,0:T(8,128)(2,1)}) %reduce-scatter.2.cloned.1.call-update) | async-done | bytes 1048592 | tf_op jit(solution)/shard_map/reduce_scatter | solution.py:115
  412.6 0.0 copy-done.1
  (10 shorter events, 0.1 us)
Async XLA Ops:
  6.5 4.7 %copy-start = (bf16[8,128,896]{2,1,0:T(8,128)(2,1)S(1)}, bf16[8,128,896]{2,1,0:T(8,128)(2,1)}, u32[]{:S(2)}) copy-start(bf16[8,128,896]{2,1,0:T(8,128)(2,1)} %param.12) | copy-start | bytes 5505028
  6.5 72.5 %all-gather.5.cloned.1.call-start = ((), (), s32[]{:S(2)}) async-start(), calls=%async_computation.3 | async-start | bytes 7798784 | tf_op jit(solution)/shard_map/all_gather | solution.py:79
  7.3 139.9 %all-gather.3.cloned.1.call-start = ((), (), s32[]{:S(2)}) async-start(), calls=%async_computation.2 | async-start | bytes 7798784 | tf_op jit(solution)/shard_map/all_gather | solution.py:80
  88.7 1.3 copy-start.3
  164.2 88.2 %copy-start.4 = (bf16[896,512]{1,0:T(8,128)(2,1)S(1)}, bf16[896,512]{1,0:T(8,128)(2,1)}, u32[]{:S(2)}) copy-start(bf16[896,512]{1,0:T(8,128)(2,1)} %param.16) | copy-start | bytes 2752516
  164.2 88.2 %all-to-all-start = ((bf16[8,4,128,896]{3,2,1,0:T(8,128)(2,1)}), bf16[8,4,128,896]{3,2,1,0:T(8,128)(2,1)}, u32[]{:S(2)}, u32[]{:S(2)}) async-start(bf16[8,4,128,896]{3,2,1,0:T(8,128)(2,1)} %stack.2), calls=%async_computation | async-start | bytes 14680064 | tf_op jit(solution)/shard_map/all_to_all | solution.py:89
  169.7 242.9 %reduce-scatter.2.cloned.1.call-start = ((), (), s32[]{:S(2)}) async-start(), calls=%async_computation.4 | async-start | bytes 9437184 | tf_op jit(solution)/shard_map/reduce_scatter | solution.py:115
  252.3 9.2 %copy-start.5 = (bf16[896,512]{1,0:T(8,128)(2,1)S(1)}, bf16[896,512]{1,0:T(8,128)(2,1)}, u32[]{:S(2)}) copy-start(bf16[896,512]{1,0:T(8,128)(2,1)} %param.15) | copy-start | bytes 2752516
  300.8 13.6 %collective-permute-start = (bf16[256,1024]{1,0:T(8,128)(2,1)}, bf16[256,1024]{1,0:T(8,128)(2,1)S(1)}, u32[]{:S(2)}, u32[]{:S(2)}) collective-permute-start(bf16[256,1024]{1,0:T(8,128)(2,1)} %bitcast.11), channel_id=1, source_target_pairs={{0,8},{8,16},{16,24},{24,32},{32,40},{40,48},{48,56},{56,64},{64,7... | collective-permute-start | bytes 1572872 | tf_op jit(solution)/shard_map/ppermute | solution.py:21
  313.4 3.2 slice-start
  329.6 2.0 copy-start.2
  361.3 51.3 %copy-start.1 = (bf16[8,128,896]{2,1,0:T(8,128)(2,1)S(1)}, bf16[8,128,896]{2,1,0:T(8,128)(2,1)}, u32[]{:S(2)}) copy-start(bf16[8,128,896]{2,1,0:T(8,128)(2,1)} %param.12) | copy-start | bytes 5505028
Sparse Core Ops, SparseCore 0:
  9.5 69.4 all-gather.4
  81.2 65.8 all-gather.2
  361.4 51.0 reduce-scatter.1
